TPU v7x, 32 devices: a whole 2x2x4 slice. The times are simulated.
32 devices in a mesh: blk: 8 (over z, x), mp: 4 (over y, core).
Axes of the slice: x: 2, y: 2, z: 4, core: 2. Of those that a mesh axis runs over, the one named last changes fastest.
Arguments:
- tokens: bfloat16 [8, 320, 7168], P('blk', 'mp'), may hold values from -6 to 6
- cotangent: bfloat16 [8, 320, 7168], P('blk', 'mp'), may hold values from -6 to 6
- gate_weight: bfloat16 [8, 7168, 512], P('blk', None, 'mp'), may hold values from -6 to 6
- up_weight: bfloat16 [8, 7168, 512], P('blk', None, 'mp'), may hold values from -6 to 6
- down_weight: bfloat16 [8, 512, 7168], P('blk', 'mp'), may hold values from -6 to 6
- mass: float32 [8], P('blk'), may hold values from 0.25 to 4
Outputs:
- gate_next: bfloat16 [8, 7168, 512], P('blk', None, 'mp')
- up_next: bfloat16 [8, 7168, 512], P('blk', None, 'mp')
- down_next: bfloat16 [8, 512, 7168], P('blk', 'mp')
- mass_next: float32 [8], P('blk')
- mass_total: float32 [], replicated
All inputs are finite; a program needn't handle non-finite values.
Results may differ from a plain program's by a relative error of at most 0.0051.
Values may be sent and summed in bfloat16 or wider, within the bound.
A program may use at most 128 MiB of HBM per device.

v0:
```python
import jax
import jax.numpy as jnp
from jax import lax
from jax.sharding import PartitionSpec as P

step_size = 0.5


def passed_along(array, axis, by):
    count = lax.axis_size(axis)
    return lax.ppermute(array, axis, [(i, (i + by) % count) for i in range(count)])


def on_device(tokens, cotangent, gate_weight, up_weight, down_weight, mass):
    whole_x, whole_dy = (
        lax.all_gather(tokens, "mp", axis=1, tiled=True),
        lax.all_gather(cotangent, "mp", axis=1, tiled=True),
    )
    inputs = whole_x[0]
    grads_out = whole_dy[0]
    gate_w = gate_weight[0]
    up_w = up_weight[0]
    down_w = down_weight[0]
    width = gate_w.shape[0]
    units = gate_w.shape[1]
    inv_d = width ** (-0.5)
    inv_h = (units * lax.axis_size("mp")) ** (-0.5)
    coeffs = (3.0, 3.0, 1.0)
    summed_mass = mass
    moving_mass = mass
    for turn in range(3):
        moving_mass = passed_along(moving_mass, "blk", 1)
        summed_mass = summed_mass + coeffs[turn] * moving_mass
    mass_next = summed_mass / 8.0
    mass_total = lax.psum(jnp.sum(mass_next), "blk")
    gate_pre = jnp.dot(inputs, gate_w, preferred_element_type=jnp.float32) * inv_d
    up_pre = jnp.dot(inputs, up_w, preferred_element_type=jnp.float32) * inv_d
    sig = jax.nn.sigmoid(gate_pre)
    hidden = (gate_pre * sig * up_pre).astype(jnp.bfloat16)
    hidden_grad = (
        lax.dot_general(
            grads_out, down_w, (((1,), (1,)), ((), ())), preferred_element_type=jnp.float32
        )
        * inv_h
    )
    gate_gp = (hidden_grad * up_pre * sig * (1.0 + gate_pre * (1.0 - sig))).astype(jnp.bfloat16)
    up_gp = (hidden_grad * gate_pre * sig).astype(jnp.bfloat16)
    contract_rows = (((0,), (0,)), ((), ()))
    down_grad = (
        lax.dot_general(hidden, grads_out, contract_rows, preferred_element_type=jnp.float32)
        * inv_h
    )
    gate_grad = (
        lax.dot_general(inputs, gate_gp, contract_rows, preferred_element_type=jnp.float32) * inv_d
    )
    up_grad = (
        lax.dot_general(inputs, up_gp, contract_rows, preferred_element_type=jnp.float32) * inv_d
    )
    weight = mass[0]
    numer_gate = (weight * (gate_w.astype(jnp.float32) - step_size * gate_grad)).astype(
        jnp.bfloat16
    )
    numer_up = (weight * (up_w.astype(jnp.float32) - step_size * up_grad)).astype(jnp.bfloat16)
    numer_down = (weight * (down_w.astype(jnp.float32) - step_size * down_grad)).astype(
        jnp.bfloat16
    )
    stacked = jnp.stack([numer_gate, numer_up, numer_down.reshape(width, units)])
    summed = stacked.astype(jnp.float32)
    moving = stacked
    for turn in range(3):
        moving = passed_along(moving, "blk", 1)
        summed = summed + coeffs[turn] * moving.astype(jnp.float32)
    result = (summed / 8.0 / mass_next[0]).astype(jnp.bfloat16)
    gate_next = result[0][None]
    up_next = result[1][None]
    down_next = result[2].reshape(units, width)[None]
    return (gate_next, up_next, down_next, mass_next, mass_total)


def solution(mesh):
    in_specs = (
        P("blk", "mp", None),
        P("blk", "mp", None),
        P("blk", None, "mp"),
        P("blk", None, "mp"),
        P("blk", "mp", None),
        P("blk"),
    )
    out_specs = (P("blk", None, "mp"), P("blk", None, "mp"), P("blk", "mp", None), P("blk"), P())
    return jax.shard_map(
        on_device, mesh=mesh, in_specs=in_specs, out_specs=out_specs, check_vma=False
    )
```

profile of v0, /device:TPU:0, one launch (start us, length us, event | category | flops | bytes accessed | tf_op | source)
XLA Modules:
  0.0 545.1 jit_solution(8592089782529909022)
XLA Ops:
  7.2 0.7 all-gather.5.cloned.1.call-update
  7.9 0.7 all-gather.3.cloned.1.call-update
  9.3 4.0 copy.15
  13.3 3.9 copy.16
  17.2 31.8 %all-gather.5.cloned.1.call-done = bf16[1,320,7168]{2,1,0:T(8,128)(2,1)} async-done(((bf16[1,80,7168]{2,1,0:T(8,128)(2,1)}), bf16[1,320,7168]{2,1,0:T(8,128)(2,1)}) %all-gather.5.cloned.1.call-update) | async-done | bytes 4587536 | tf_op jit(solution)/shard_map/all_gather | solution.py:16
  49.0 3.8 fusion.35
  52.8 0.5 copy-done.4
  53.3 1.3 fusion.30
  54.6 32.7 %all-gather.3.cloned.1.call-done = bf16[1,320,7168]{2,1,0:T(8,128)(2,1)} async-done(((bf16[1,80,7168]{2,1,0:T(8,128)(2,1)}), bf16[1,320,7168]{2,1,0:T(8,128)(2,1)}) %all-gather.3.cloned.1.call-update) | async-done | bytes 4587536 | tf_op jit(solution)/shard_map/all_gather | solution.py:17
  87.3 4.9 fusion.10
  92.2 3.9 stack_reshape.3
  96.1 2.8 copy.17
  98.9 4.4 fusion.25
  103.3 4.0 fusion.12
  107.4 1.5 fusion.11
  108.9 0.9 pad_maximum_fusion
  109.7 0.4 copy-done.2
  110.1 1.5 collective-permute-start
  111.6 122.0 %collective-permute-done = bf16[3,7168,128]{1,2,0:T(8,128)(2,1)S(1)} collective-permute-done((bf16[3,7168,128]{1,2,0:T(8,128)(2,1)S(1)}, bf16[3,7168,128]{1,2,0:T(8,128)(2,1)S(1)}, u32[]{:S(2)}, u32[]{:S(2)}) %collective-permute-start) | collective-permute-done | bytes 5505056 | tf_op jit(solution)/shard_map/ppermute | solution.py:11
  233.6 2.4 copy-done.9
  236.0 122.7 %collective-permute-done.1 = bf16[3,7168,128]{1,2,0:T(8,128)(2,1)} collective-permute-done((bf16[3,7168,128]{1,2,0:T(8,128)(2,1)S(1)}, bf16[3,7168,128]{1,2,0:T(8,128)(2,1)}, u32[]{:S(2)}, u32[]{:S(2)}) %collective-permute-start.1) | collective-permute-done | bytes 5505056 | tf_op jit(solution)/shard_map/ppermute | solution.py:11
  358.7 122.2 %collective-permute-done.3 = f32[1]{0:T(128)} collective-permute-done((f32[1]{0:T(128)}, f32[1]{0:T(128)}, u32[]{:S(2)}, u32[]{:S(2)}) %collective-permute-start.3) | collective-permute-done | bytes 36 | tf_op jit(solution)/shard_map/ppermute | solution.py:11
  481.6 0.1 collective-permute-start.4
  481.6 6.6 %collective-permute-done.4 = f32[1]{0:T(128)} collective-permute-done((f32[1]{0:T(128)}, f32[1]{0:T(128)}, u32[]{:S(2)}, u32[]{:S(2)}) %collective-permute-start.4) | collective-permute-done | bytes 36 | tf_op jit(solution)/shard_map/ppermute | solution.py:11
  488.8 6.6 %collective-permute-done.5 = f32[1]{0:T(128)} collective-permute-done((f32[1]{0:T(128)}, f32[1]{0:T(128)}, u32[]{:S(2)}, u32[]{:S(2)}) %collective-permute-start.5) | collective-permute-done | bytes 36 | tf_op jit(solution)/shard_map/ppermute | solution.py:11
  496.0 18.5 %psum.7 = f32[]{:T(128)} all-reduce(f32[]{:T(128)} %bitcast.10), channel_id=1, replica_groups=mesh['blk'=8,'mp'=4] {'blk'}, use_global_device_ids=true, to_apply=%region_0.0 | all-reduce | flops 1 | bytes 8 | tf_op jit(solution)/shard_map/psum | solution.py:35
  514.5 8.7 %divide_convert_fusion = bf16[3,7168,128]{1,2,0:T(8,128)(2,1)S(1)} fusion(bf16[3,7168,128]{1,2,0:T(8,128)(2,1)} %collective-permute-done.2, bf16[3,7168,128]{1,2,0:T(8,128)(2,1)} %collective-permute-done.1, bf16[3,7168,128]{1,2,0:T(8,128)(2,1)} %copy-done.9, f32[]{:T(128)} %bitcast.10, bf16[1,7168,128]{1,2,0:T(8,128)(2,1)S(1)} %copy.17, ...), kind=kLoop, calls=%fused_computation | loop fusion | flops 38535168 | bytes 27525124 | tf_op jit(solution)/shard_map/convert_element_type | solution.py:73
  523.2 2.6 fusion.46
  525.8 3.3 copy.18
  529.1 1.7 broadcast_in_dim_reshape_squeeze.3
  530.8 4.0 copy.19
  534.9 2.3 copy.20
  (29 shorter events, 0.2 us)
Async XLA Ops:
  7.2 41.8 %all-gather.5.cloned.1.call-start = ((), (), s32[]{:S(2)}) async-start(), calls=%async_computation.1 | async-start | bytes 5734400 | tf_op jit(solution)/shard_map/all_gather | solution.py:16
  7.9 79.4 %all-gather.3.cloned.1.call-start = ((), (), s32[]{:S(2)}) async-start(), calls=%async_computation | async-start | bytes 5734400 | tf_op jit(solution)/shard_map/all_gather | solution.py:17
  9.3 39.7 %copy-start.3 = (bf16[1,7168,128]{2,1,0:T(8,128)(2,1)S(1)}, bf16[1,7168,128]{2,1,0:T(8,128)(2,1)}, u32[]{:S(2)}) copy-start(bf16[1,7168,128]{2,1,0:T(8,128)(2,1)} %param.8) | copy-start | bytes 5505028
  49.0 3.8 copy-start
  49.0 4.3 copy-start.4
  53.3 34.0 %copy-start.5 = (bf16[1,128,7168]{2,1,0:T(8,128)(2,1)S(1)}, bf16[1,128,7168]{2,1,0:T(8,128)(2,1)}, u32[]{:S(2)}) copy-start(bf16[1,128,7168]{2,1,0:T(8,128)(2,1)} %param.10) | copy-start | bytes 5505028
  98.9 4.4 copy-start.7
  98.9 8.4 %slice-start = ((s8[4587520]{0:T(1024)(128)(4,1)}), s8[4194304]{0:T(1024)(128)(4,1)S(1)}, s32[]{:S(2)}) async-start(s8[4587520]{0:T(1024)(128)(4,1)} %bitcast.69), calls=%async_computation.2 | async-start | bytes 8388608
  103.3 4.0 slice-start.1
  103.3 4.0 copy-start.6
  107.3 1.5 copy-start.1
  108.9 1.2 copy-start.2
  110.1 123.5 %collective-permute-start = (bf16[3,7168,128]{1,2,0:T(8,128)(2,1)S(1)}, bf16[3,7168,128]{1,2,0:T(8,128)(2,1)S(1)}, u32[]{:S(2)}, u32[]{:S(2)}) collective-permute-start(bf16[3,7168,128]{1,2,0:T(8,128)(2,1)S(1)} %pad_maximum_fusion), channel_id=1, source_target_pairs={{0,4},{4,8},{8,12},{12,16},{16,20},{20,24},{24,28},{28,0},{1,5},{5... | collective-permute-start | bytes 16515080 | tf_op jit(solution)/shard_map/ppermute | solution.py:11
  233.6 2.4 copy-start.9
  236.0 122.8 %collective-permute-start.1 = (bf16[3,7168,128]{1,2,0:T(8,128)(2,1)S(1)}, bf16[3,7168,128]{1,2,0:T(8,128)(2,1)}, u32[]{:S(2)}, u32[]{:S(2)}) collective-permute-start(bf16[3,7168,128]{1,2,0:T(8,128)(2,1)S(1)} %collective-permute-done), channel_id=1, source_target_pairs={{0,4},{4,8},{8,12},{12,16},{16,20},{20,24},{24,28},{28,0},{1,5},{5... | collective-permute-start | bytes 16515080 | tf_op jit(solution)/shard_map/ppermute | solution.py:11
  358.7 155.8 %collective-permute-start.2 = (bf16[3,7168,128]{1,2,0:T(8,128)(2,1)}, bf16[3,7168,128]{1,2,0:T(8,128)(2,1)}, u32[]{:S(2)}, u32[]{:S(2)}) collective-permute-start(bf16[3,7168,128]{1,2,0:T(8,128)(2,1)} %collective-permute-done.1), channel_id=1, source_target_pairs={{0,4},{4,8},{8,12},{12,16},{16,20},{20,24},{24,28},{28,0},{1,5},{5... | collective-permute-start | bytes 16515080 | tf_op jit(solution)/shard_map/ppermute | solution.py:11
  358.7 122.2 %collective-permute-start.3 = (f32[1]{0:T(128)}, f32[1]{0:T(128)}, u32[]{:S(2)}, u32[]{:S(2)}) collective-permute-start(f32[1]{0:T(128)} %param.11), channel_id=1, source_target_pairs={{0,4},{4,8},{8,12},{12,16},{16,20},{20,24},{24,28},{28,0},{1,5},{5... | collective-permute-start | bytes 20 | tf_op jit(solution)/shard_map/ppermute | solution.py:11
  481.6 6.6 %collective-permute-start.4 = (f32[1]{0:T(128)}, f32[1]{0:T(128)}, u32[]{:S(2)}, u32[]{:S(2)}) collective-permute-start(f32[1]{0:T(128)} %collective-permute-done.3), channel_id=1, source_target_pairs={{0,4},{4,8},{8,12},{12,16},{16,20},{20,24},{24,28},{28,0},{1,5},{5... | collective-permute-start | bytes 20 | tf_op jit(solution)/shard_map/ppermute | solution.py:11
  488.7 6.6 %collective-permute-start.5 = (f32[1]{0:T(128)}, f32[1]{0:T(128)}, u32[]{:S(2)}, u32[]{:S(2)}) collective-permute-start(f32[1]{0:T(128)} %collective-permute-done.4), channel_id=1, source_target_pairs={{0,4},{4,8},{8,12},{12,16},{16,20},{20,24},{24,28},{28,0},{1,5},{5... | collective-permute-start | bytes 20 | tf_op jit(solution)/shard_map/ppermute | solution.py:11
  530.8 4.0 copy-start.8
Sparse Core Ops, SparseCore 0:
  9.5 39.4 all-gather.4
  50.5 36.6 all-gather.2
where the time goes:
time: 546 us; the launch traced here: 545 us
  waiting for transfers between devices  446 us (82%)
  local copies, waits for them, and re-layouts  31.7 us (6%)
  matrix products  19.9 us (4%)
  blocking collectives  18.5 us (3%)
  between operations  17.8 us (3%)
  other arithmetic  9.55 us (2%)
    ppermute x6, waiting for transfers between devices, passed_along(): lax.ppermute(array, axis, [(i, (i + by) % count) for i in range(count)])  380 us
    all_gather x1, waiting for transfers between devices, on_device(): lax.all_gather(cotangent, 'mp', axis=1, tiled=True)  32.7 us
    all_gather x1, waiting for transfers between devices, on_device(): lax.all_gather(tokens, 'mp', axis=1, tiled=True)  31.8 us
    psum x1, blocking collectives, on_device(): mass_total = lax.psum(jnp.sum(mass_next), 'blk')  18.5 us
    unnamed x28, local copies, waits for them, and re-layouts  17.4 us
  transfers between devices with their start and end apart: 8, of which 7 were waited for; matrix products, arithmetic and copies ran while one was open for 2% of the time, Pallas kernels for 0%

commit v1 on v0

v1 whole, which is shorter than its diff:
```python
import functools

import jax
import jax.numpy as jnp
from jax import lax
from jax.experimental import pallas as pl
from jax.experimental.pallas import tpu as pltpu
from jax.sharding import PartitionSpec as P

step_size = 0.5
MESH = pl.DeviceIdType.MESH
f32 = jnp.float32
bf16 = jnp.bfloat16


def largest_cut(width, most):
    return max(c for c in range(1, most + 1) if width % (c * 128) == 0)


def kernel(
    reps, mp, pieces, chunks,
    tok, cot, wg, wu, wd, mass_s, mass_v,
    gate_o, up_o, down_o, mass_o,
    xy, wgu, wdv, nb, eb, cb, sb, rb, mbuf, acc_gu, acc_h, gpre, hid_t,
    load_sem, own_send, own_recv, far_send, far_recv, fwd_send, fwd_recv,
    m_send, m_recv, e_send, e_recv, c1_send, c_send, c_recv, s_send, r_recv, o_sem,
):
    me = lax.axis_index("blk")
    my = lax.axis_index("mp")
    rows = tok.shape[0]
    width = tok.shape[1]
    units = wg.shape[1]
    inv_d = width ** (-0.5)
    inv_h = (units * mp) ** (-0.5)
    piece = width // pieces
    span = width // chunks
    far = mp // 2 - 1
    odd = lax.rem(me, 2) == 1
    even = lax.rem(me, 2) == 0
    partner = me + 1 - 2 * lax.rem(me, 2)
    ahead = lax.rem(me + 2, reps)
    sibling = my + 1 - 2 * lax.rem(my, 2)

    sources = (tok, cot)
    loads = [
        pltpu.make_async_copy(wg, wgu.at[:, pl.ds(0, units)], load_sem.at[0]),
        pltpu.make_async_copy(wu, wgu.at[:, pl.ds(units, units)], load_sem.at[1]),
        pltpu.make_async_copy(wd, wdv, load_sem.at[2]),
    ]
    mine = pl.ds(pl.multiple_of(my * rows, rows), rows)
    for a in range(2):
        loads.append(pltpu.make_async_copy(sources[a], xy.at[a, mine, :], load_sem.at[3 + a]))
    for load in loads:
        load.start()

    barrier = pltpu.get_barrier_semaphore()

    def greet_blk(d, carry):
        pl.semaphore_signal(
            barrier, inc=1, device_id={"blk": lax.rem(me + d, reps)}, device_id_type=MESH
        )
        return carry

    def greet_mp(d, carry):
        pl.semaphore_signal(
            barrier, inc=1, device_id={"mp": lax.rem(my + d, mp)}, device_id_type=MESH
        )
        return carry

    lax.fori_loop(1, reps, greet_blk, 0)
    lax.fori_loop(1, mp, greet_mp, 0)
    pl.semaphore_wait(barrier, reps - 1 + mp - 1)

    def cols_of(p):
        return pl.ds(pl.multiple_of(p * piece, 128), piece)

    def rows_of(owner):
        return pl.ds(pl.multiple_of(owner * rows, rows), rows)

    def own_copy(a, p):
        return pltpu.make_async_remote_copy(
            src_ref=sources[a].at[:, cols_of(p)],
            dst_ref=xy.at[a, mine, cols_of(p)],
            send_sem=own_send.at[a, p],
            recv_sem=own_recv.at[a, p],
            device_id={"mp": sibling},
            device_id_type=MESH,
        )

    def far_copy(a, q, p):
        return pltpu.make_async_remote_copy(
            src_ref=sources[a].at[:, cols_of(p)],
            dst_ref=xy.at[a, mine, cols_of(p)],
            send_sem=far_send.at[a, q, p],
            recv_sem=far_recv.at[a, q, p],
            device_id={"mp": lax.rem(my + 2 * (q + 1), mp)},
            device_id_type=MESH,
        )

    def fwd_copy(a, q, p):
        owner = lax.rem(my + mp - 2 * (q + 1), mp)
        block = xy.at[a, rows_of(owner), cols_of(p)]
        return pltpu.make_async_remote_copy(
            src_ref=block,
            dst_ref=block,
            send_sem=fwd_send.at[a, q, p],
            recv_sem=fwd_recv.at[a, q, p],
            device_id={"mp": sibling},
            device_id_type=MESH,
        )

    def issue(p, carry):
        for a in range(2):
            for q in range(far):
                far_copy(a, q, p).start()
            own_copy(a, p).start()
        return carry

    lax.fori_loop(0, pieces, issue, 0)

    def mass_copy(d):
        return pltpu.make_async_remote_copy(
            src_ref=mass_v,
            dst_ref=mbuf.at[me],
            send_sem=m_send.at[d],
            recv_sem=m_recv.at[d],
            device_id={"blk": lax.rem(me + d, reps)},
            device_id_type=MESH,
        )

    def mass_start(d, carry):
        mass_copy(d).start()
        return carry

    lax.fori_loop(1, reps, mass_start, 0)
    mbuf[me] = mass_v[...]

    acc_gu[...] = jnp.zeros_like(acc_gu)
    acc_h[...] = jnp.zeros_like(acc_h)
    for load in loads:
        load.wait()

    def gather_step(t, carry):
        @pl.when(t < pieces)
        def _():
            for a in range(2):
                for q in range(far):
                    far_copy(a, q, t).wait_recv()
                    fwd_copy(a, q, t).start()

        @pl.when(t >= 1)
        def _():
            p = t - 1
            for a in range(2):
                own_copy(a, p).wait_recv()
                for q in range(far):
                    fwd_copy(a, q, p).wait_recv()
            cols = cols_of(p)
            acc_gu[...] += jnp.dot(xy[0, :, cols], wgu[cols, :], preferred_element_type=f32)
            acc_h[...] += lax.dot_general(
                xy[1, :, cols], wdv[:, cols], (((1,), (1,)), ((), ())),
                preferred_element_type=f32,
            )

        return carry

    lax.fori_loop(0, pieces + 1, gather_step, 0)

    gate_pre = acc_gu[:, :units] * inv_d
    up_pre = acc_gu[:, units:] * inv_d
    sig = jax.nn.sigmoid(gate_pre)
    hidden = gate_pre * sig * up_pre
    hid_t[...] = hidden.T.astype(bf16)
    hidden_grad = acc_h[...] * inv_h
    gpre[:, :units] = (hidden_grad * up_pre * sig * (1.0 + gate_pre * (1.0 - sig))).astype(bf16)
    gpre[:, units:] = (hidden_grad * gate_pre * sig).astype(bf16)

    def mass_wait(d, carry):
        mass_copy(d).wait()
        return carry

    lax.fori_loop(1, reps, mass_wait, 0)
    mass_next = (
        mbuf[me]
        + 3.0 * mbuf[lax.rem(me + reps - 1, reps)]
        + 3.0 * mbuf[lax.rem(me + reps - 2, reps)]
        + mbuf[lax.rem(me + reps - 3, reps)]
    ) / 8.0
    mass_o[0] = mass_next
    mass_o[1] = jnp.sum(mbuf[...], axis=0)
    weight = mass_s[0]
    scale = (1.0 / (8.0 * mass_next))[0:1, :]

    def span_of(j):
        return pl.ds(pl.multiple_of(j * span, 128), span)

    def remote(src, dst, send, recv, target):
        return pltpu.make_async_remote_copy(
            src_ref=src, dst_ref=dst, send_sem=send, recv_sem=recv,
            device_id={"blk": target}, device_id_type=MESH,
        )

    def pair_copy(j):
        return remote(nb.at[j], eb.at[j], e_send.at[j], e_recv.at[j], partner)

    def odd_ahead(j):
        return remote(nb.at[j], cb.at[j], c1_send.at[j], c_recv.at[j], ahead)

    def odd_across(j):
        return remote(cb.at[j], cb.at[j], c_send.at[j], c_recv.at[j], partner)

    def even_ahead(j):
        return remote(eb.at[j], cb.at[j], c_send.at[j], c_recv.at[j], ahead)

    def sum_copy(j):
        return remote(sb.at[j], rb.at[j], s_send.at[j], r_recv.at[j], ahead)

    def outs(j):
        at = span_of(j)
        return (
            pltpu.make_async_copy(wgu.at[at, pl.ds(0, units)], gate_o.at[at, :], o_sem.at[0, j]),
            pltpu.make_async_copy(
                wgu.at[at, pl.ds(units, units)], up_o.at[at, :], o_sem.at[1, j]
            ),
            pltpu.make_async_copy(wdv.at[:, at], down_o.at[:, at], o_sem.at[2, j]),
        )

    def mix_step(t, carry):
        @pl.when(t < chunks)
        def _():
            j = t
            at = span_of(j)
            grads = lax.dot_general(
                xy[0, :, at], gpre[...], (((0,), (0,)), ((), ())), preferred_element_type=f32
            )
            numer = (weight * (wgu[at, :].astype(f32) - (step_size * inv_d) * grads)).astype(bf16)
            nb[j, 0] = numer[:, :units]
            nb[j, 1] = numer[:, units:]
            down_grad = jnp.dot(hid_t[...], xy[1, :, at], preferred_element_type=f32)
            down = (
                weight * (wdv[:, at].astype(f32) - (step_size * inv_h) * down_grad)
            ).astype(bf16)
            for b in range(span // units):
                nb[j, 2, b * units : (b + 1) * units, :] = down[:, b * units : (b + 1) * units]
            pair_copy(j).start()

            @pl.when(odd & (lax.rem(j, 2) == 1))
            def _():
                odd_ahead(j).start()

        @pl.when((t >= 2) & (t < chunks + 2))
        def _():
            j = t - 2
            pair_copy(j).wait_recv()

            @pl.when(even & (lax.rem(j, 2) == 0))
            def _():
                even_ahead(j).start()

            @pl.when(odd)
            def _():
                sb[j] = (3.0 * nb[j].astype(f32) + eb[j].astype(f32)).astype(bf16)
                sum_copy(j).start()

            @pl.when(odd & (lax.rem(j, 2) == 1))
            def _():
                odd_ahead(j).wait_recv()
                odd_across(j).start()

        @pl.when((t >= 4) & (t < chunks + 4) & even)
        def _():
            j = t - 4
            even_ahead(j).wait_recv()
            sb[j] = (
                3.0 * (nb[j].astype(f32) + eb[j].astype(f32)) + cb[j].astype(f32)
            ).astype(bf16)
            sum_copy(j).start()

        @pl.when(t >= 7)
        def _():
            j = t - 7
            sum_copy(j).wait_recv()
            at = span_of(j)
            near = jnp.where(odd, 3.0, 0.0).astype(f32)

            def mixed(i):
                total = nb[j, i].astype(f32) + near * eb[j, i].astype(f32)
                return ((total + rb[j, i].astype(f32)) * scale).astype(bf16)

            wgu[at, :units] = mixed(0)
            wgu[at, units:] = mixed(1)
            down = mixed(2)
            for b in range(span // units):
                here = pl.ds(pl.multiple_of(j * span + b * units, 128), units)
                wdv[:, here] = down[b * units : (b + 1) * units, :]
            for out in outs(j):
                out.start()

        return carry

    lax.fori_loop(0, chunks + 7, mix_step, 0)

    def drain_gather(p, carry):
        for a in range(2):
            own_copy(a, p).wait_send()
            for q in range(far):
                far_copy(a, q, p).wait_send()
                fwd_copy(a, q, p).wait_send()
        return carry

    lax.fori_loop(0, pieces, drain_gather, 0)

    def drain_mix(j, carry):
        pair_copy(j).wait_send()
        sum_copy(j).wait_send()

        @pl.when(odd & (lax.rem(j, 2) == 1))
        def _():
            odd_ahead(j).wait_send()
            odd_across(j).wait_send()

        @pl.when(even & (lax.rem(j, 2) == 0))
        def _():
            even_ahead(j).wait_send()

        for out in outs(j):
            out.wait()
        return carry

    lax.fori_loop(0, chunks, drain_mix, 0)


def on_device(reps, mp, tokens, cotangent, gate_weight, up_weight, down_weight, mass):
    rows, width = tokens.shape[1:]
    units = gate_weight.shape[2]
    pieces = largest_cut(width, 7)
    chunks = largest_cut(width, 14)
    span = width // chunks
    far = max(mp // 2 - 1, 1)
    dma = pltpu.SemaphoreType.DMA
    slab = pltpu.VMEM((chunks, 3, span, units), bf16)
    anywhere = pl.BlockSpec(memory_space=pl.ANY)
    vmem = pl.BlockSpec(memory_space=pltpu.VMEM)
    gate, up, down, masses = pl.pallas_call(
        functools.partial(kernel, reps, mp, pieces, chunks),
        out_shape=(
            jax.ShapeDtypeStruct((width, units), bf16),
            jax.ShapeDtypeStruct((width, units), bf16),
            jax.ShapeDtypeStruct((units, width), bf16),
            jax.ShapeDtypeStruct((2, 8, 128), f32),
        ),
        in_specs=[anywhere] * 5 + [pl.BlockSpec(memory_space=pltpu.SMEM), vmem],
        out_specs=(anywhere, anywhere, anywhere, vmem),
        scratch_shapes=[
            pltpu.VMEM((2, rows * mp, width), bf16),
            pltpu.VMEM((width, 2 * units), bf16),
            pltpu.VMEM((units, width), bf16),
            slab, slab, slab, slab, slab,
            pltpu.VMEM((reps, 8, 128), f32),
            pltpu.VMEM((rows * mp, 2 * units), f32),
            pltpu.VMEM((rows * mp, units), f32),
            pltpu.VMEM((rows * mp, 2 * units), bf16),
            pltpu.VMEM((units, rows * mp), bf16),
            dma((5,)),
            dma((2, pieces)), dma((2, pieces)),
            dma((2, far, pieces)), dma((2, far, pieces)),
            dma((2, far, pieces)), dma((2, far, pieces)),
            dma((reps,)), dma((reps,)),
            dma((chunks,)), dma((chunks,)), dma((chunks,)), dma((chunks,)),
            dma((chunks,)), dma((chunks,)), dma((chunks,)),
            dma((3, chunks)),
        ],
        compiler_params=pltpu.CompilerParams(
            collective_id=0, has_side_effects=True, vmem_limit_bytes=60 * 1024 * 1024
        ),
        name="push_step",
    )(
        tokens[0], cotangent[0], gate_weight[0], up_weight[0], down_weight[0],
        mass, jnp.broadcast_to(mass[0], (8, 128)),
    )
    return gate[None], up[None], down[None], masses[0, 0, :1], masses[1, 0, 0]


def solution(mesh):
    in_specs = (
        P("blk", "mp", None),
        P("blk", "mp", None),
        P("blk", None, "mp"),
        P("blk", None, "mp"),
        P("blk", "mp", None),
        P("blk"),
    )
    out_specs = (P("blk", None, "mp"), P("blk", None, "mp"), P("blk", "mp", None), P("blk"), P())
    return jax.shard_map(
        functools.partial(on_device, mesh.shape["blk"], mesh.shape["mp"]),
        mesh=mesh, in_specs=in_specs, out_specs=out_specs, check_vma=False,
    )
```

time: 546 us -> 271 us (0.50)
  waiting for transfers between devices: 446 us -> 0 us
  Pallas kernels: 0 us -> 262 us
  local copies, waits for them, and re-layouts: 31.7 us -> 8.16 us
  matrix products: 19.9 us -> 0 us
  blocking collectives: 18.5 us -> 0 us
  between operations: 17.8 us -> 1.29 us
  other arithmetic: 9.55 us -> 0 us
    ppermute x6 -> x0, waiting for transfers between devices: 380 us -> none  [passed_along(): lax.ppermute(array, axis, [(i, (i + by) % count) for i in range(count)])]
    pallas_call x0 -> x1, Pallas kernels: none -> 262 us  [on_device(): pl.pallas_call(functools.partial(kernel, reps, mp, pieces, chunks), out_s...]
    all_gather x2 -> x0, waiting for transfers between devices: 64.4 us -> none  [the longest x1 32.7 us: on_device(): lax.all_gather(cotangent, 'mp', axis=1, tiled=True)]
    dot_general x6 -> x0, matrix products: 19.9 us -> none  [the longest x1 4.94 us: on_device(): lax.dot_general(hidden, grads_out, contract_rows, preferred_element_type=...]
    psum x1 -> x0, blocking collectives: 18.5 us -> none  [on_device(): mass_total = lax.psum(jnp.sum(mass_next), 'blk')]
    unnamed x28 -> x7, local copies, waits for them, and re-layouts: 17.4 us -> 6.37 us
    convert_element_type x1 -> x0, other arithmetic: 8.7 us -> none  [on_device(): result = (summed / 8.0 / mass_next[0]).astype(jnp.bfloat16)]
    another operation x3 -> x0, local copies, waits for them, and re-layouts: 8.42 us -> none  [the longest x2 6.69 us: on_device(): jnp.stack([numer_gate, numer_up, numer_down.reshape(width, units)])]
  transfers between devices with their start and end apart: 8 -> 0, of which waited for: 7 -> 0; matrix products, arithmetic and copies ran while one was open for 2% -> 0% of each run, Pallas kernels for 0% -> 0%
where the time goes in v1:
time: 271 us
  Pallas kernels  262 us (97%)
  local copies, waits for them, and re-layouts  8.16 us (3%)
    pallas_call x1, Pallas kernels, on_device(): pl.pallas_call(functools.partial(kernel, reps, mp, pieces, chunks), out_s...  262 us
    unnamed x7, local copies, waits for them, and re-layouts  6.37 us

profile of v1, /device:TPU:0, one launch (start us, length us, event | category | flops | bytes accessed | tf_op | source)
XLA Modules:
  0.0 271.1 jit_solution(5427202410687844272)
XLA Ops:
  1.3 0.6 broadcast_in_dim.12.mass_v
  1.9 261.7 %push_step.1 = (bf16[7168,128]{1,0:T(8,128)(2,1)}, bf16[7168,128]{1,0:T(8,128)(2,1)}, bf16[128,7168]{1,0:T(8,128)(2,1)}, f32[2,8,128]{2,1,0:T(8,128)}) custom-call(bf16[80,7168]{1,0:T(8,128)(2,1)} %bitcast.18, bf16[80,7168]{1,0:T(8,128)(2,1)} %bitcast.19, bf16[7168,128]{1,0:T(8,128)(2,1)} %bitcast.12, bf16[7168,128]{1,0:T(8,128)(2,1)} %bitcast.13, ...), custom_call_target="tpu_custom_call" | custom-call | tf_op jit(solution)/shard_map/push_step/pallas_call | solution.py:344
  263.5 1.2 fusion
  264.7 0.0 copy-start.1
  264.7 3.0 %copy.15 = bf16[1,7168,128]{2,1,0:T(8,128)(2,1)} copy(bf16[1,7168,128]{2,1,0:T(8,128)(2,1)} %bitcast.17) | data formatting | bytes 3670016
  267.7 0.0 copy-done.1
  267.7 0.0 copy-start
  267.7 1.2 copy.16
  268.9 0.9 copy-done
  269.9 1.2 copy.17
Async XLA Ops:
  264.7 3.0 %copy-start.1 = (bf16[7168,128]{1,0:T(8,128)(2,1)S(1)}, bf16[7168,128]{1,0:T(8,128)(2,1)}, u32[]{:S(2)}) copy-start(bf16[7168,128]{1,0:T(8,128)(2,1)} %get-tuple-element.10) | copy-start | bytes 5505028
  267.7 2.2 copy-start

commit v2 on v1

--- a/solution.py
+++ b/solution.py
@@ -8,6 +8,7 @@
 from jax.sharding import PartitionSpec as P
 
 step_size = 0.5
+lag_b, lag_c, lag_d = 2, 3, 6
 MESH = pl.DeviceIdType.MESH
 f32 = jnp.float32
 bf16 = jnp.bfloat16
@@ -207,7 +208,7 @@
         return remote(nb.at[j], cb.at[j], c1_send.at[j], c_recv.at[j], ahead)
 
     def odd_across(j):
-        return remote(cb.at[j], cb.at[j], c_send.at[j], c_recv.at[j], partner)
+        return remote(cb.at[j], eb.at[j], c_send.at[j], e_recv.at[j], partner)
 
     def even_ahead(j):
         return remote(eb.at[j], cb.at[j], c_send.at[j], c_recv.at[j], ahead)
@@ -242,43 +243,60 @@
             ).astype(bf16)
             for b in range(span // units):
                 nb[j, 2, b * units : (b + 1) * units, :] = down[:, b * units : (b + 1) * units]
-            pair_copy(j).start()
-
-            @pl.when(odd & (lax.rem(j, 2) == 1))
+            via_odd = lax.rem(j, 2) == 1
+
+            @pl.when(odd & via_odd)
             def _():
                 odd_ahead(j).start()
 
-        @pl.when((t >= 2) & (t < chunks + 2))
-        def _():
-            j = t - 2
-            pair_copy(j).wait_recv()
-
-            @pl.when(even & (lax.rem(j, 2) == 0))
-            def _():
-                even_ahead(j).start()
+            @pl.when(even | jnp.logical_not(via_odd))
+            def _():
+                pair_copy(j).start()
+
+        @pl.when((t >= lag_b) & (t < chunks + lag_b))
+        def _():
+            j = t - lag_b
+            via_odd = lax.rem(j, 2) == 1
 
             @pl.when(odd)
             def _():
+                pair_copy(j).wait_recv()
                 sb[j] = (3.0 * nb[j].astype(f32) + eb[j].astype(f32)).astype(bf16)
                 sum_copy(j).start()
 
-            @pl.when(odd & (lax.rem(j, 2) == 1))
+            @pl.when(odd & via_odd)
             def _():
                 odd_ahead(j).wait_recv()
+                cb[j] = (3.0 * nb[j].astype(f32) + cb[j].astype(f32)).astype(bf16)
                 odd_across(j).start()
 
-        @pl.when((t >= 4) & (t < chunks + 4) & even)
-        def _():
-            j = t - 4
-            even_ahead(j).wait_recv()
-            sb[j] = (
-                3.0 * (nb[j].astype(f32) + eb[j].astype(f32)) + cb[j].astype(f32)
-            ).astype(bf16)
+            @pl.when(even & jnp.logical_not(via_odd))
+            def _():
+                pair_copy(j).wait_recv()
+                even_ahead(j).start()
+
+        @pl.when((t >= lag_c) & (t < chunks + lag_c) & even)
+        def _():
+            j = t - lag_c
+            via_odd = lax.rem(j, 2) == 1
+
+            @pl.when(via_odd)
+            def _():
+                odd_across(j).wait_recv()
+                sb[j] = (3.0 * nb[j].astype(f32) + eb[j].astype(f32)).astype(bf16)
+
+            @pl.when(jnp.logical_not(via_odd))
+            def _():
+                even_ahead(j).wait_recv()
+                sb[j] = (
+                    3.0 * (nb[j].astype(f32) + eb[j].astype(f32)) + cb[j].astype(f32)
+                ).astype(bf16)
+
             sum_copy(j).start()
 
-        @pl.when(t >= 7)
-        def _():
-            j = t - 7
+        @pl.when(t >= lag_d)
+        def _():
+            j = t - lag_d
             sum_copy(j).wait_recv()
             at = span_of(j)
             near = jnp.where(odd, 3.0, 0.0).astype(f32)
@@ -298,7 +316,7 @@
 
         return carry
 
-    lax.fori_loop(0, chunks + 7, mix_step, 0)
+    lax.fori_loop(0, chunks + lag_d, mix_step, 0)
 
     def drain_gather(p, carry):
         for a in range(2):
@@ -311,8 +329,11 @@
     lax.fori_loop(0, pieces, drain_gather, 0)
 
     def drain_mix(j, carry):
-        pair_copy(j).wait_send()
         sum_copy(j).wait_send()
+
+        @pl.when(even | (lax.rem(j, 2) == 0))
+        def _():
+            pair_copy(j).wait_send()
 
         @pl.when(odd & (lax.rem(j, 2) == 1))
         def _():
@@ -334,7 +355,7 @@
     rows, width = tokens.shape[1:]
     units = gate_weight.shape[2]
     pieces = largest_cut(width, 7)
-    chunks = largest_cut(width, 14)
+    chunks = largest_cut(width, 28)
     span = width // chunks
     far = max(mp // 2 - 1, 1)
     dma = pltpu.SemaphoreType.DMA
@@ -371,7 +392,7 @@
             dma((3, chunks)),
         ],
         compiler_params=pltpu.CompilerParams(
-            collective_id=0, has_side_effects=True, vmem_limit_bytes=60 * 1024 * 1024
+            collective_id=0, has_side_effects=True, vmem_limit_bytes=48 * 1024 * 1024
         ),
         name="push_step",
     )(

time: 271 us -> 260 us (0.959)
  Pallas kernels: 262 us -> 251 us
    pallas_call x1, Pallas kernels: 262 us -> 251 us  [on_device(): pl.pallas_call(functools.partial(kernel, reps, mp, pieces, chunks), out_s...]
    unnamed x7 -> x9, local copies, waits for them, and re-layouts: 6.37 us -> 7.13 us
where the time goes in v2:
time: 260 us
  Pallas kernels  251 us (97%)
  local copies, waits for them, and re-layouts  7.65 us (3%)
    pallas_call x1, Pallas kernels, on_device(): pl.pallas_call(functools.partial(kernel, reps, mp, pieces, chunks), out_s...  251 us
    unnamed x9, local copies, waits for them, and re-layouts  7.13 us

profile of v2, /device:TPU:0, one launch (start us, length us, event | category | flops | bytes accessed | tf_op | source)
XLA Modules:
  0.0 259.5 jit_solution(10068313783784080370)
XLA Ops:
  1.3 0.0 copy-start
  1.3 1.2 copy-done
  2.6 0.0 copy-start.1
  2.6 1.3 copy-done.1
  3.8 250.6 %push_step.1 = (bf16[7168,128]{1,0:T(8,128)(2,1)S(1)}, bf16[7168,128]{1,0:T(8,128)(2,1)S(1)}, bf16[128,7168]{1,0:T(8,128)(2,1)}, f32[2,8,128]{2,1,0:T(8,128)S(1)}) custom-call(bf16[80,7168]{1,0:T(8,128)(2,1)S(1)} %bitcast.14, bf16[80,7168]{1,0:T(8,128)(2,1)S(1)} %bitcast.15, bf16[7168,128]{1,0:T(8,128)(2,1)} %bitcast.16, bf16[7168,128]{1,0:T(8,128)(2,1)} %bitcast.17, ...), custom_call_target="tpu_custom_call" | custom-call | tf_op jit(solution)/shard_map/push_step/pallas_call | solution.py:365
  254.4 0.5 fusion
  254.9 1.2 copy.15
  256.2 0.0 copy-start.2
  256.2 1.2 copy.16
  257.4 0.9 copy-done.2
  258.3 1.2 copy.17
  (1 shorter events, 0.0 us)
Async XLA Ops:
  1.3 1.3 copy-start
  2.6 1.3 copy-start.1
  256.2 2.2 copy-start.2

commit v3 on v2

--- a/solution.py
+++ b/solution.py
@@ -8,7 +8,7 @@
 from jax.sharding import PartitionSpec as P
 
 step_size = 0.5
-lag_b, lag_c, lag_d = 2, 3, 6
+lag_b, lag_c, lag_d = 3, 4, 8
 MESH = pl.DeviceIdType.MESH
 f32 = jnp.float32
 bf16 = jnp.bfloat16
@@ -192,6 +192,9 @@
     weight = mass_s[0]
     scale = (1.0 / (8.0 * mass_next))[0:1, :]
 
+    def through_odd(j):
+        return (lax.rem(j, 2) == 1) | (j == chunks // 2)
+
     def span_of(j):
         return pl.ds(pl.multiple_of(j * span, 128), span)
 
@@ -243,7 +246,7 @@
             ).astype(bf16)
             for b in range(span // units):
                 nb[j, 2, b * units : (b + 1) * units, :] = down[:, b * units : (b + 1) * units]
-            via_odd = lax.rem(j, 2) == 1
+            via_odd = through_odd(j)
 
             @pl.when(odd & via_odd)
             def _():
@@ -256,7 +259,7 @@
         @pl.when((t >= lag_b) & (t < chunks + lag_b))
         def _():
             j = t - lag_b
-            via_odd = lax.rem(j, 2) == 1
+            via_odd = through_odd(j)
 
             @pl.when(odd)
             def _():
@@ -278,7 +281,7 @@
         @pl.when((t >= lag_c) & (t < chunks + lag_c) & even)
         def _():
             j = t - lag_c
-            via_odd = lax.rem(j, 2) == 1
+            via_odd = through_odd(j)
 
             @pl.when(via_odd)
             def _():
@@ -331,16 +334,16 @@
     def drain_mix(j, carry):
         sum_copy(j).wait_send()
 
-        @pl.when(even | (lax.rem(j, 2) == 0))
+        @pl.when(even | jnp.logical_not(through_odd(j)))
         def _():
             pair_copy(j).wait_send()
 
-        @pl.when(odd & (lax.rem(j, 2) == 1))
+        @pl.when(odd & through_odd(j))
         def _():
             odd_ahead(j).wait_send()
             odd_across(j).wait_send()
 
-        @pl.when(even & (lax.rem(j, 2) == 0))
+        @pl.when(even & jnp.logical_not(through_odd(j)))
         def _():
             even_ahead(j).wait_send()
 
@@ -392,7 +395,7 @@
             dma((3, chunks)),
         ],
         compiler_params=pltpu.CompilerParams(
-            collective_id=0, has_side_effects=True, vmem_limit_bytes=48 * 1024 * 1024
+            collective_id=0, has_side_effects=True, vmem_limit_bytes=53 * 1024 * 1024
         ),
         name="push_step",
     )(

time: 260 us -> 255 us (0.981)
  Pallas kernels: 251 us -> 246 us
    pallas_call x1, Pallas kernels: 251 us -> 246 us  [on_device(): pl.pallas_call(functools.partial(kernel, reps, mp, pieces, chunks), out_s...]
    unnamed x9 -> x7, local copies, waits for them, and re-layouts: 7.13 us -> 6.37 us
where the time goes in v3:
time: 255 us; the launch traced here: 254 us
  Pallas kernels  246 us (96%)
  local copies, waits for them, and re-layouts  6.89 us (3%)
    pallas_call x1, Pallas kernels, on_device(): pl.pallas_call(functools.partial(kernel, reps, mp, pieces, chunks), out_s...  246 us
    unnamed x7, local copies, waits for them, and re-layouts  6.37 us

profile of v3, /device:TPU:0, one launch (start us, length us, event | category | flops | bytes accessed | tf_op | source)
XLA Modules:
  0.0 254.4 jit_solution(17005497359631515618)
XLA Ops:
  1.3 246.2 %push_step.1 = (bf16[7168,128]{1,0:T(8,128)(2,1)}, bf16[7168,128]{1,0:T(8,128)(2,1)}, bf16[128,7168]{1,0:T(8,128)(2,1)}, f32[2,8,128]{2,1,0:T(8,128)S(1)}) custom-call(bf16[80,7168]{1,0:T(8,128)(2,1)} %bitcast.18, bf16[80,7168]{1,0:T(8,128)(2,1)} %bitcast.19, bf16[7168,128]{1,0:T(8,128)(2,1)} %bitcast.12, bf16[7168,128]{1,0:T(8,128)(2,1)} %bitcast.13, ...), custom_call_target="tpu_custom_call" | custom-call | tf_op jit(solution)/shard_map/push_step/pallas_call | solution.py:368
  247.5 0.5 fusion
  248.1 0.0 copy-start.1
  248.1 3.0 %copy.15 = bf16[1,7168,128]{2,1,0:T(8,128)(2,1)} copy(bf16[1,7168,128]{2,1,0:T(8,128)(2,1)} %bitcast.17) | data formatting | bytes 3670016
  251.0 0.0 copy-done.1
  251.0 0.0 copy-start
  251.0 1.2 copy.16
  252.3 0.9 copy-done
  253.2 1.2 copy.17
  (1 shorter events, 0.0 us)
Async XLA Ops:
  248.1 3.0 %copy-start.1 = (bf16[7168,128]{1,0:T(8,128)(2,1)S(1)}, bf16[7168,128]{1,0:T(8,128)(2,1)}, u32[]{:S(2)}) copy-start(bf16[7168,128]{1,0:T(8,128)(2,1)} %get-tuple-element.10) | copy-start | bytes 5505028
  251.0 2.2 copy-start

commit v4 on v3

--- a/solution.py
+++ b/solution.py
@@ -261,17 +261,17 @@
             j = t - lag_b
             via_odd = through_odd(j)
 
+            @pl.when(odd & via_odd)
+            def _():
+                odd_ahead(j).wait_recv()
+                cb[j] = (3.0 * nb[j].astype(f32) + cb[j].astype(f32)).astype(bf16)
+                odd_across(j).start()
+
             @pl.when(odd)
             def _():
                 pair_copy(j).wait_recv()
                 sb[j] = (3.0 * nb[j].astype(f32) + eb[j].astype(f32)).astype(bf16)
                 sum_copy(j).start()
-
-            @pl.when(odd & via_odd)
-            def _():
-                odd_ahead(j).wait_recv()
-                cb[j] = (3.0 * nb[j].astype(f32) + cb[j].astype(f32)).astype(bf16)
-                odd_across(j).start()
 
             @pl.when(even & jnp.logical_not(via_odd))
             def _():

time: 255 us -> 255 us (level)
  no operation moved by 1% of the time
where the time goes in v4:
time: 255 us; the launch traced here: 254 us
  Pallas kernels  246 us (96%)
  local copies, waits for them, and re-layouts  6.89 us (3%)
    pallas_call x1, Pallas kernels, on_device(): pl.pallas_call(functools.partial(kernel, reps, mp, pieces, chunks), out_s...  246 us
    unnamed x7, local copies, waits for them, and re-layouts  6.37 us

profile of v4, /device:TPU:0, one launch (start us, length us, event | category | flops | bytes accessed | tf_op | source)
XLA Modules:
  0.0 254.4 jit_solution(14029937168868217140)
XLA Ops:
  1.3 246.2 %push_step.1 = (bf16[7168,128]{1,0:T(8,128)(2,1)}, bf16[7168,128]{1,0:T(8,128)(2,1)}, bf16[128,7168]{1,0:T(8,128)(2,1)}, f32[2,8,128]{2,1,0:T(8,128)S(1)}) custom-call(bf16[80,7168]{1,0:T(8,128)(2,1)} %bitcast.18, bf16[80,7168]{1,0:T(8,128)(2,1)} %bitcast.19, bf16[7168,128]{1,0:T(8,128)(2,1)} %bitcast.12, bf16[7168,128]{1,0:T(8,128)(2,1)} %bitcast.13, ...), custom_call_target="tpu_custom_call" | custom-call | tf_op jit(solution)/shard_map/push_step/pallas_call | solution.py:368
  247.5 0.5 fusion
  248.1 0.0 copy-start.1
  248.1 3.0 %copy.15 = bf16[1,7168,128]{2,1,0:T(8,128)(2,1)} copy(bf16[1,7168,128]{2,1,0:T(8,128)(2,1)} %bitcast.17) | data formatting | bytes 3670016
  251.0 0.0 copy-done.1
  251.0 0.0 copy-start
  251.0 1.2 copy.16
  252.3 0.9 copy-done
  253.2 1.2 copy.17
  (1 shorter events, 0.0 us)
Async XLA Ops:
  248.1 3.0 %copy-start.1 = (bf16[7168,128]{1,0:T(8,128)(2,1)S(1)}, bf16[7168,128]{1,0:T(8,128)(2,1)}, u32[]{:S(2)}) copy-start(bf16[7168,128]{1,0:T(8,128)(2,1)} %get-tuple-element.10) | copy-start | bytes 5505028
  251.0 2.2 copy-start
